TPU v7x, 512 devices: a whole 4x8x8 slice. The times are simulated.
512 devices in a mesh: cons: 4 (over y_hi), ty: 8 (over x, y_lo), tx: 16 (over z, core).
Axes of the slice: x: 4, y: 8 (y_hi: 4, y_lo: 2; y = y_hi * 2 + y_lo), z: 8, core: 2. Of those that a mesh axis runs over, the one named last changes fastest.
Arguments:
- elevation: float32 [8, 2, 1152, 8192], P('cons', None, 'ty', 'tx'), may hold values from -6 to 6
- equilibrium: float32 [8, 2, 1152, 8192], P('cons', None, 'ty', 'tx'), may hold values from -5 to 5
- depth: float32 [1152, 8192], P('ty', 'tx'), may hold values from 0.1 to 1
- land_mask: int32 [1152, 8192], P('ty', 'tx'), may hold values 0 or 1
- friction_prev: float32 [1152, 8192], P('ty', 'tx'), may hold values from 0.3 to 3
Outputs:
- elevation_out: float32 [8, 2, 1152, 8192], P('cons', None, 'ty', 'tx')
- friction: float32 [1152, 8192], P('ty', 'tx')
All inputs are finite; a program needn't handle non-finite values. No bound on the sum of `land_mask` on one device may be relied on, other than what follows from the above.
Results may differ from a plain program's by a relative error of at most 0.00002.
Values sent between devices are 32-bit elements; how exact they have to be, the bound alone decides.
A program may use at most 64 MiB of HBM per device.

v0:
```python
import math

import jax
import jax.numpy as jnp
from jax import lax
from jax.sharding import PartitionSpec as P

OMEGA_TABLE = (1.0, 1.0351, 0.9582, 1.0379, 0.5181, 0.4816, 0.5164, 0.4454)
AY_SCALE = 0.5
THETA = 0.05
DRAG = 0.5
BACKGROUND = 0.01


def passed_along(value, axis, steps):
    count = lax.axis_size(axis)
    pairs = [(source, (source + steps) % count) for source in range(count)]
    return lax.ppermute(value, axis, pairs)


def passed_along_2(block, axis, distance):
    devices = range(lax.axis_size(axis))
    route = [(i - distance, i) for i in devices if i - distance in devices]
    return lax.ppermute(block, axis, route)


def latitude_factor(rows, total):
    lat = (-60.0 + 120.0 * (rows.astype(jnp.float32) + 0.5) / total) * (math.pi / 180.0)
    return 0.5 / jnp.cos(lat)


def momentum(num_re, num_im, fric, omega, face_mask):
    denom = fric * fric + omega * omega
    return (
        face_mask * (num_re * fric + num_im * omega) / denom,
        face_mask * (num_im * fric - num_re * omega) / denom,
    )


def ahead_rims(planes):
    east_col = passed_along(planes[:, :, 0], "tx", -1)
    north_row = passed_along_2(planes[:, 0, :], "ty", -1)
    return (east_col, north_row)


def forward_rims(planes):
    east_col, north_row = ahead_rims(planes)
    east_view = jnp.concatenate([planes[:, :, 1:], east_col[:, :, None]], axis=2)
    north_view = jnp.concatenate([planes[:, 1:, :], north_row[:, None, :]], axis=1)
    return (east_view, north_view)


def backward_rims(trans_u, trans_v):
    west_col = passed_along(trans_u[..., :, -1], "tx", 1)
    south_row = passed_along_2(trans_v[..., -1, :], "ty", 1)
    west_u = jnp.concatenate([west_col[..., None], trans_u[..., :, :-1]], axis=-1)
    south_v = jnp.concatenate([south_row[..., None, :], trans_v[..., :-1, :]], axis=-2)
    return (west_u, south_v)


def finish(eta, trans_u, west_u, trans_v, south_v, omega, ax_rows, maskf, depth):
    div = ax_rows * (trans_u - west_u) + AY_SCALE * (trans_v - south_v)
    res = jnp.stack([-omega * eta[:, 1] + div[:, 0], omega * eta[:, 0] + div[:, 1]], axis=1)
    eta_new = maskf * (eta - THETA * res)
    cu = 0.5 * (trans_u + west_u)
    cv = 0.5 * (trans_v + south_v)
    term = 0.5 * (
        cu[:, 0] * cu[:, 0] + cu[:, 1] * cu[:, 1] + cv[:, 0] * cv[:, 0] + cv[:, 1] * cv[:, 1]
    )
    variance_part = jnp.sum(term, axis=0) / (depth * depth)
    return (eta_new, variance_part)


def sweep_core(eta, zeta, zeta_east, zeta_north, fric, fric_east, fric_north, omega, statics):
    ax_rows, maskf, mu_face, mv_face, hu_face, hv_face, depth = statics
    grad_x = ax_rows * (zeta_east - zeta)
    grad_y = AY_SCALE * (zeta_north - zeta)
    fric_u = 0.5 * (fric + fric_east)
    fric_v = 0.5 * (fric + fric_north)
    u_re, u_im = momentum(-hu_face * grad_x[:, 0], -hu_face * grad_x[:, 1], fric_u, omega, mu_face)
    v_re, v_im = momentum(-hv_face * grad_y[:, 0], -hv_face * grad_y[:, 1], fric_v, omega, mv_face)
    trans_u = jnp.stack([u_re, u_im], axis=1)
    trans_v = jnp.stack([v_re, v_im], axis=1)
    west_u, south_v = backward_rims(trans_u, trans_v)
    return finish(eta, trans_u, west_u, trans_v, south_v, omega, ax_rows, maskf, depth)


def compute_friction(variance_local, depth):
    variance_total = lax.psum(variance_local, "cons")
    return DRAG * jnp.sqrt(variance_total + BACKGROUND) / depth


def body(elevation, equilibrium, depth, land_mask, friction_prev):
    kdev, two, rows_dev, cols_dev = elevation.shape
    first_cons = lax.axis_index("cons") * kdev
    omega = lax.dynamic_slice_in_dim(jnp.array(OMEGA_TABLE, dtype=jnp.float32), first_cons, kdev)[
        :, None, None
    ]
    rows = lax.axis_index("ty") * rows_dev + jnp.arange(rows_dev, dtype=jnp.int32)
    ax_rows = latitude_factor(rows, rows_dev * lax.axis_size("ty"))[:, None]
    maskf = land_mask.astype(jnp.float32)
    planes_count = kdev * 2
    zeta = elevation - equilibrium
    planes = jnp.concatenate(
        [
            zeta.reshape(planes_count, rows_dev, cols_dev),
            friction_prev[None],
            depth[None],
            maskf[None],
        ],
        axis=0,
    )
    east_view, north_view = forward_rims(planes)
    depth_east = east_view[planes_count + 1]
    depth_north = north_view[planes_count + 1]
    mask_east = east_view[planes_count + 2]
    mask_north = north_view[planes_count + 2]
    statics = (
        ax_rows,
        maskf,
        maskf * mask_east,
        maskf * mask_north,
        0.5 * (depth + depth_east),
        0.5 * (depth + depth_north),
        depth,
    )
    eta_one, variance_local = sweep_core(
        elevation,
        zeta,
        east_view[:planes_count].reshape(kdev, 2, rows_dev, cols_dev),
        north_view[:planes_count].reshape(kdev, 2, rows_dev, cols_dev),
        friction_prev,
        east_view[planes_count],
        north_view[planes_count],
        omega,
        statics,
    )
    friction = compute_friction(variance_local, depth)
    zeta_two = eta_one - equilibrium
    planes_two = jnp.concatenate(
        [zeta_two.reshape(planes_count, rows_dev, cols_dev), friction[None]], axis=0
    )
    east_two, north_two = forward_rims(planes_two)
    eta_two, unused = sweep_core(
        eta_one,
        zeta_two,
        east_two[:planes_count].reshape(kdev, 2, rows_dev, cols_dev),
        north_two[:planes_count].reshape(kdev, 2, rows_dev, cols_dev),
        friction,
        east_two[planes_count],
        north_two[planes_count],
        omega,
        statics,
    )
    return (eta_two, friction)


def solution(mesh):
    return jax.shard_map(
        body,
        mesh=mesh,
        in_specs=(
            P("cons", None, "ty", "tx"),
            P("cons", None, "ty", "tx"),
            P("ty", "tx"),
            P("ty", "tx"),
            P("ty", "tx"),
        ),
        out_specs=(P("cons", None, "ty", "tx"), P("ty", "tx")),
        check_vma=False,
    )
```

profile of v0, /device:TPU:1, one launch (start us, length us, event | category | flops | bytes accessed | tf_op | source)
XLA Modules:
  0.0 136.4 jit_solution(13368709324180972753)
XLA Ops:
  7.2 1.7 %fusion.62 = (f32[144,512]{1,0:T(8,128)}, f32[1,144,512]{2,1,0:T(8,128)S(1)}) fusion(s32[144,512]{1,0:T(8,128)} %param.9), kind=kLoop, calls=%fused_computation.150 | loop fusion | flops 73728 | bytes 884736 | tf_op jit(solution)/shard_map/convert_element_type | solution.py:101
  8.9 1.9 %sub.52 = f32[2,2,144,512]{3,2,1,0:T(8,128)S(1)} subtract(f32[2,2,144,512]{3,2,1,0:T(8,128)} %param.6, f32[2,2,144,512]{3,2,1,0:T(8,128)} %param.7) | non-fusion elementwise | flops 294912 | bytes 3538944 | tf_op jit(solution)/shard_map/sub | solution.py:103
  10.9 1.3 collective-permute-start.2
  12.4 0.9 slice_reduce_fusion
  13.3 6.9 %collective-permute-start = (f32[7,144]{1,0:T(8,128)}, f32[7,144]{1,0:T(8,128)}, u32[]{:S(2)}, u32[]{:S(2)}) collective-permute-start(f32[7,144]{1,0:T(8,128)} %slice_reduce_fusion), channel_id=1, source_target_pairs={{0,15},{1,0},{2,1},{3,2},{4,3},{5,4},{6,5},{7,6},{8,7},{9,8},{10,9... | collective-permute-start | bytes 12104 | tf_op jit(solution)/shard_map/ppermute | solution.py:18
  20.2 1.3 dynamic-slice_negate_fusion
  22.1 1.8 %slice.206 = f32[7,143,512]{2,1,0:T(8,128)} slice(f32[7,144,512]{2,1,0:T(8,128)S(1)} %pad_maximum_fusion), slice={[0:7], [1:144], [0:512]} | slice | bytes 4100096 | tf_op jit(solution)/shard_map/slice | solution.py:49
  23.9 1.9 %slice.196 = f32[7,144,511]{2,1,0:T(8,128)} slice(f32[7,144,512]{2,1,0:T(8,128)S(1)} %pad_maximum_fusion), slice={[0:7], [0:144], [1:512]} | slice | bytes 4120704 | tf_op jit(solution)/shard_map/slice | solution.py:48
  25.8 1.9 %copy.28 = f32[7,144,1]{2,1,0:T(8,128)} copy(f32[7,144,1]{1,0,2:T(8,128)} %bitcast.4) | data formatting | bytes 8064 | tf_op jit(solution)/shard_map/broadcast_in_dim | solution.py:48
  27.6 1.6 %fusion.14 = f32[4,144,512]{2,1,0:T(8,128)S(1)} fusion(f32[7,144,511]{2,1,0:T(8,128)} %slice.196, f32[7,144,1]{2,1,0:T(8,128)} %copy.28), kind=kLoop, calls=%fused_computation.49 | loop fusion | flops 294912 | bytes 3244032 | tf_op jit(solution)/shard_map/concatenate | solution.py:48
  30.0 1.5 %fusion.60 = (f32[144,512]{1,0:T(8,128)S(1)}, f32[144,512]{1,0:T(8,128)S(1)}, f32[144,512]{1,0:T(8,128)S(1)}, f32[144,512]{1,0:T(8,128)S(1)}, f32[144,512]{1,0:T...) fusion(f32[144,512]{1,0:T(8,128)} %param.10, ...), kind=kLoop, calls=%fused_computation.149 | loop fusion | flops 1548288 | bytes 7372800 | tf_op jit(solution)/shard_map/mul | solution.py:33
  32.8 0.8 add_divide_fusion.7
  33.9 1.1 fusion.12
  35.1 4.3 %collective-permute-start.3 = (f32[2,2,512]{2,1,0:T(2,128)S(1)}, f32[2,2,512]{2,1,0:T(2,128)S(1)}, u32[]{:S(2)}, u32[]{:S(2)}) collective-permute-start(f32[2,2,512]{2,1,0:T(2,128)S(1)} %bitcast.102), channel_id=1, source_target_pairs={{0,16},{16,32},{32,48},{48,64},{64,80},{80,96},{96,112},{1,17},{17... | collective-permute-start | bytes 24584 | tf_op jit(solution)/shard_map/ppermute | solution.py:24
  39.4 1.1 fusion.8
  40.7 3.4 %add_multiply_fusion.1 = (f32[2,2,144,512]{3,2,1,0:T(8,128)S(1)}, f32[2,2,144,512]{3,2,1,0:T(8,128)}, f32[2,2,144,512]{3,2,1,0:T(8,128)S(1)}) fusion(f32[2,1,144,512]{3,2,1,0:T(8,128)S(1)} %get-tuple-element.22, f32[2,1,144,512]{3,2,1,0:T(8,128)S(1)} %get-tuple-element.21, f32[2,2,144,511]{3,2,1,0:T(8,128)} %fusion.12, f32[2,2,144,1]{3,2,1,0:T(8,128)S(1)} %copy.29, ...), kind=kLoop, calls=%fused_computation.61 | loop fusion | flops 3833856 | bytes 8258112 | tf_op jit(solution)/shard_map/mul | solution.py:65
  46.2 0.9 copy-done.7
  47.2 1.5 %fusion.56 = (f32[2,2,144,512]{3,2,1,0:T(8,128)S(1)}, f32[2,2,144,512]{3,2,1,0:T(8,128)}) fusion(f32[2,2,144,512]{3,2,1,0:T(8,128)S(1)} %copy-done.7, f32[2,2,144,512]{3,2,1,0:T(8,128)S(1)} %copy-done.4, f32[2,1,144,512]{3,2,1,0:T(8,128)S(1)} %get-tuple-element.28, f32[2,1,144,512]{3,2,1,0:T(8,128)S(1)} %get-tuple-element.27, f32[144,512]{1,0:T(8,128)S(1)} %copy-done.10), kind=kLoop, calls=%fused_computation.147 | loop fusion | flops 1474560 | bytes 6193152 | tf_op jit(solution)/shard_map/sub | solution.py:139
  48.7 52.7 %all-reduce.2.cloned.1.call-done = f32[144,512]{1,0:T(8,128)} async-done(((f32[144,512]{1,0:T(8,128)}), f32[144,512]{1,0:T(8,128)}) %all-reduce.2.cloned.1.call-update) | async-done | bytes 294928 | tf_op jit(solution)/shard_map/psum | solution.py:89
  101.4 1.1 multiply_divide_fusion
  102.7 1.6 %fusion.1 = f32[5,144,511]{2,1,0:T(8,128)} fusion(f32[4,144,512]{2,1,0:T(8,128)S(1)} %bitcast.82, f32[1,144,512]{2,1,0:T(8,128)S(1)} %bitcast.88), kind=kLoop, calls=%fused_computation.32 | loop fusion | flops 367920 | bytes 2946240 | tf_op jit(solution)/shard_map/concatenate | solution.py:140
  104.6 2.7 %collective-permute-start.4 = (f32[5,144]{1,0:T(8,128)S(1)}, f32[5,144]{1,0:T(8,128)S(1)}, u32[]{:S(2)}, u32[]{:S(2)}) collective-permute-start(f32[5,144]{1,0:T(8,128)S(1)} %fusion.25), channel_id=1, source_target_pairs={{0,15},{1,0},{2,1},{3,2},{4,3},{5,4},{6,5},{7,6},{8,7},{9,8},{10,9... | collective-permute-start | bytes 8648 | tf_op jit(solution)/shard_map/ppermute | solution.py:18
  107.3 1.3 collective-permute-start.6
  108.6 1.3 collective-permute-done.4
  110.0 1.5 %fusion.3 = f32[4,144,512]{2,1,0:T(8,128)S(1)} fusion(f32[5,144,511]{2,1,0:T(8,128)} %fusion.1, f32[5,144,1]{2,1,0:T(8,128)S(1)} %copy.31), kind=kLoop, calls=%fused_computation.38 | loop fusion | flops 294912 | bytes 2654208 | tf_op jit(solution)/shard_map/concatenate | solution.py:48
  113.3 0.8 add_divide_fusion.3
  114.6 2.5 %collective-permute-start.5 = (f32[2,2,144]{2,1,0:T(2,128)S(1)}, f32[2,2,144]{2,1,0:T(2,128)S(1)}, u32[]{:S(2)}, u32[]{:S(2)}) collective-permute-start(f32[2,2,144]{2,1,0:T(2,128)S(1)} %fusion.27), channel_id=1, source_target_pairs={{0,1},{1,2},{2,3},{3,4},{4,5},{5,6},{6,7},{7,8},{8,9},{9,10},{10,1... | collective-permute-start | bytes 6920 | tf_op jit(solution)/shard_map/ppermute | solution.py:18
  117.0 4.2 %collective-permute-start.7 = (f32[2,2,512]{2,1,0:T(2,128)S(1)}, f32[2,2,512]{2,1,0:T(2,128)}, u32[]{:S(2)}, u32[]{:S(2)}) collective-permute-start(f32[2,2,512]{2,1,0:T(2,128)S(1)} %bitcast.103), channel_id=1, source_target_pairs={{0,16},{16,32},{32,48},{48,64},{64,80},{80,96},{96,112},{1,17},{17... | collective-permute-start | bytes 24584 | tf_op jit(solution)/shard_map/ppermute | solution.py:24
  121.2 1.1 fusion.4
  122.9 1.5 %copy.32 = f32[2,2,144,1]{3,2,1,0:T(8,128)} copy(f32[2,2,144,1]{2,1,0,3:T(2,128)} %bitcast.106) | data formatting | bytes 4608 | tf_op jit(solution)/shard_map/broadcast_in_dim | solution.py:56
  125.1 2.1 %fusion.7 = f32[2,2,144,512]{3,2,1,0:T(8,128)S(1)} fusion(f32[2,1,144,512]{3,2,1,0:T(8,128)S(1)} %get-tuple-element.43, f32[2,1,144,512]{3,2,1,0:T(8,128)S(1)} %get-tuple-element.44, f32[2,1,144,512]{3,2,1,0:T(8,128)S(1)} %get-tuple-element.18, f32[2,1,144,512]{3,2,1,0:T(8,128)S(1)} %get-tuple-element.17, f32[2,2,144,511]{3,2,1,0:T(8,128)S(1)} %fusion.9, ...), kind=kLoop, calls=%fused_computation.42 | loop fusion | flops 2654208 | bytes 5898816 | tf_op jit(solution)/shard_map/add | solution.py:62
  128.2 1.3 fusion.18
  (91 shorter events, 10.6 us)
Async XLA Ops:
  7.2 94.2 %all-reduce.2.cloned.1.call-start = ((), (), s32[]{:S(2)}) async-start(), calls=%async_computation | async-start | bytes 589824 | tf_op jit(solution)/shard_map/psum | solution.py:89
  8.9 1.9 %copy-start.6 = (f32[144,512]{1,0:T(8,128)S(1)}, f32[144,512]{1,0:T(8,128)}, u32[]{:S(2)}) copy-start(f32[144,512]{1,0:T(8,128)} %param.8) | copy-start | bytes 884740
  8.9 1.9 %copy-start.9 = (f32[144,512]{1,0:T(8,128)S(1)}, f32[144,512]{1,0:T(8,128)}, u32[]{:S(2)}) copy-start(f32[144,512]{1,0:T(8,128)} %param.10) | copy-start | bytes 884740
  10.9 18.4 %collective-permute-start.2 = (f32[7,512]{1,0:T(8,128)S(1)}, f32[7,512]{1,0:T(8,128)}, u32[]{:S(2)}, u32[]{:S(2)}) collective-permute-start(f32[7,512]{1,0:T(8,128)S(1)} %bitcast.99), channel_id=1, source_target_pairs={{16,0},{32,16},{48,32},{64,48},{80,64},{96,80},{112,96},{17,1},{33... | collective-permute-start | bytes 43016 | tf_op jit(solution)/shard_map/ppermute | solution.py:24
  13.3 12.4 %collective-permute-start = (f32[7,144]{1,0:T(8,128)}, f32[7,144]{1,0:T(8,128)}, u32[]{:S(2)}, u32[]{:S(2)}) collective-permute-start(f32[7,144]{1,0:T(8,128)} %slice_reduce_fusion), channel_id=1, source_target_pairs={{0,15},{1,0},{2,1},{3,2},{4,3},{5,4},{6,5},{7,6},{8,7},{9,8},{10,9... | collective-permute-start | bytes 12104 | tf_op jit(solution)/shard_map/ppermute | solution.py:18
  25.8 4.2 %copy-start.1 = (f32[7,144,511]{2,1,0:T(8,128)S(1)}, f32[7,144,511]{2,1,0:T(8,128)}, u32[]{:S(2)}) copy-start(f32[7,144,511]{2,1,0:T(8,128)} %slice.196) | copy-start | bytes 6181060
  27.6 2.4 %copy-start = (f32[7,143,512]{2,1,0:T(8,128)S(1)}, f32[7,143,512]{2,1,0:T(8,128)}, u32[]{:S(2)}) copy-start(f32[7,143,512]{2,1,0:T(8,128)} %slice.206) | copy-start | bytes 6150148
  31.5 1.1 copy-start.12
  31.5 1.1 copy-start.14
  31.5 1.1 copy-start.16
  31.6 1.1 copy-start.18
  31.6 0.6 copy-start.20
  35.1 5.4 %collective-permute-start.1 = (f32[2,2,144]{2,1,0:T(2,128)S(1)}, f32[2,2,144]{2,1,0:T(2,128)S(1)}, u32[]{:S(2)}, u32[]{:S(2)}) collective-permute-start(f32[2,2,144]{2,1,0:T(2,128)S(1)} %fusion.29), channel_id=1, source_target_pairs={{0,1},{1,2},{2,3},{3,4},{4,5},{5,6},{6,7},{7,8},{8,9},{9,10},{10,1... | collective-permute-start | bytes 6920 | tf_op jit(solution)/shard_map/ppermute | solution.py:18
  35.1 5.6 %collective-permute-start.3 = (f32[2,2,512]{2,1,0:T(2,128)S(1)}, f32[2,2,512]{2,1,0:T(2,128)S(1)}, u32[]{:S(2)}, u32[]{:S(2)}) collective-permute-start(f32[2,2,512]{2,1,0:T(2,128)S(1)} %bitcast.102), channel_id=1, source_target_pairs={{0,16},{16,32},{32,48},{48,64},{64,80},{80,96},{96,112},{1,17},{17... | collective-permute-start | bytes 24584 | tf_op jit(solution)/shard_map/ppermute | solution.py:24
  44.1 1.3 copy-start.8
  44.4 1.5 %copy-start.4 = (f32[2,2,144,512]{3,2,1,0:T(8,128)S(1)}, f32[2,2,144,512]{3,2,1,0:T(8,128)}, u32[]{:S(2)}) copy-start(f32[2,2,144,512]{3,2,1,0:T(8,128)} %param.6) | copy-start | bytes 3538948
  44.4 1.5 %copy-start.22 = (f32[2]{0:T(128)S(1)}, f32[2]{0:T(128)}, u32[]{:S(2)}) copy-start(f32[2]{0:T(128)} %get-tuple-element.47) | copy-start | bytes 28
  45.9 1.3 copy-start.7
  45.9 1.3 copy-start.10
  102.5 9.3 %copy-start.3 = (f32[144,512]{1,0:T(8,128)}, f32[144,512]{1,0:T(8,128)S(1)}, u32[]{:S(2)}) copy-start(f32[144,512]{1,0:T(8,128)S(1)} %multiply_divide_fusion) | copy-start | bytes 884740
  104.6 5.3 %collective-permute-start.4 = (f32[5,144]{1,0:T(8,128)S(1)}, f32[5,144]{1,0:T(8,128)S(1)}, u32[]{:S(2)}, u32[]{:S(2)}) collective-permute-start(f32[5,144]{1,0:T(8,128)S(1)} %fusion.25), channel_id=1, source_target_pairs={{0,15},{1,0},{2,1},{3,2},{4,3},{5,4},{6,5},{7,6},{8,7},{9,8},{10,9... | collective-permute-start | bytes 8648 | tf_op jit(solution)/shard_map/ppermute | solution.py:18
  107.3 4.5 %collective-permute-start.6 = (f32[5,512]{1,0:T(8,128)S(1)}, f32[5,512]{1,0:T(8,128)S(1)}, u32[]{:S(2)}, u32[]{:S(2)}) collective-permute-start(f32[5,512]{1,0:T(8,128)S(1)} %bitcast.100), channel_id=1, source_target_pairs={{16,0},{32,16},{48,32},{64,48},{80,64},{96,80},{112,96},{17,1},{33... | collective-permute-start | bytes 30728 | tf_op jit(solution)/shard_map/ppermute | solution.py:24
  110.0 1.7 %copy-start.2 = (f32[5,144,511]{2,1,0:T(8,128)S(1)}, f32[5,144,511]{2,1,0:T(8,128)}, u32[]{:S(2)}) copy-start(f32[5,144,511]{2,1,0:T(8,128)} %fusion.1) | copy-start | bytes 4415044
  112.1 1.0 copy-start.13
  112.1 1.0 copy-start.15
  112.1 1.1 copy-start.17
  112.1 1.2 copy-start.19
  114.6 7.7 %collective-permute-start.5 = (f32[2,2,144]{2,1,0:T(2,128)S(1)}, f32[2,2,144]{2,1,0:T(2,128)S(1)}, u32[]{:S(2)}, u32[]{:S(2)}) collective-permute-start(f32[2,2,144]{2,1,0:T(2,128)S(1)} %fusion.27), channel_id=1, source_target_pairs={{0,1},{1,2},{2,3},{3,4},{4,5},{5,6},{6,7},{7,8},{8,9},{9,10},{10,1... | collective-permute-start | bytes 6920 | tf_op jit(solution)/shard_map/ppermute | solution.py:18
  117.0 7.4 %collective-permute-start.7 = (f32[2,2,512]{2,1,0:T(2,128)S(1)}, f32[2,2,512]{2,1,0:T(2,128)}, u32[]{:S(2)}, u32[]{:S(2)}) collective-permute-start(f32[2,2,512]{2,1,0:T(2,128)S(1)} %bitcast.103), channel_id=1, source_target_pairs={{0,16},{16,32},{32,48},{48,64},{64,80},{80,96},{96,112},{1,17},{17... | collective-permute-start | bytes 24584 | tf_op jit(solution)/shard_map/ppermute | solution.py:24
  125.1 2.1 %copy-start.5 = (f32[2,2,144,512]{3,2,1,0:T(8,128)S(1)}, f32[2,2,144,512]{3,2,1,0:T(8,128)}, u32[]{:S(2)}) copy-start(f32[2,2,144,512]{3,2,1,0:T(8,128)} %get-tuple-element.7) | copy-start | bytes 3538948
  125.1 2.1 %copy-start.23 = (f32[2]{0:T(128)S(1)}, f32[2]{0:T(128)}, u32[]{:S(2)}) copy-start(f32[2]{0:T(128)} %get-tuple-element.47) | copy-start | bytes 28
  127.2 1.0 copy-start.11
  (3 other events, 1.8 us)
Sparse Core Ops, SparseCore 0:
  45.3 56.0 all-reduce.1
where the time goes:
time: 137 us; the launch traced here: 136 us
  waiting for transfers between devices  54.2 us (40%)
  other arithmetic  30.5 us (22%)
  starting transfers between devices  23 us (17%)
  between operations  14.5 us (11%)
  local copies, waits for them, and re-layouts  14.2 us (10%)
    psum x1, waiting for transfers between devices, compute_friction(): variance_total = lax.psum(variance_local, 'cons')  52.7 us
    ppermute x4, starting transfers between devices, passed_along(): return lax.ppermute(value, axis, pairs)  12 us
    ppermute x4, starting transfers between devices, passed_along_2(): return lax.ppermute(block, axis, route)  11 us
    unnamed x56, local copies, waits for them, and re-layouts  4.38 us
    mul x1, other arithmetic, finish(): cu = 0.5 * (trans_u + west_u)  3.39 us
    concatenate x2, other arithmetic, forward_rims(): jnp.concatenate([planes[:, :, 1:], east_col[:, :, None]], axis=2)  3.17 us
  transfers between devices with their start and end apart: 9, of which 3 were waited for; matrix products, arithmetic and copies ran while one was open for 13% of the time, Pallas kernels for 0%

commit v1 on v0

v1 whole, which is shorter than its diff:
```python
import functools
import math

import jax
import jax.numpy as jnp
from jax import lax
from jax.experimental import pallas as pl
from jax.experimental.pallas import tpu as pltpu
from jax.sharding import PartitionSpec as P

OMEGA_TABLE = (1.0, 1.0351, 0.9582, 1.0379, 0.5181, 0.4816, 0.5164, 0.4454)
AY_SCALE = 0.5
THETA = 0.05
DRAG = 0.5
BACKGROUND = 0.01

MESH = pl.DeviceIdType.MESH
LANES = 128
PAD = 8
CHUNKS = 3


def latitude_factor(rows, total):
    lat = (-60.0 + 120.0 * (rows.astype(jnp.float32) + 0.5) / total) * (math.pi / 180.0)
    return 0.5 / jnp.cos(lat)


def rate_of(total, depth):
    inverse = 1.0 / depth
    return DRAG * jnp.sqrt(0.125 * total * (inverse * inverse) + BACKGROUND) * inverse


def face_flow(d_re, d_im, rate, scale, omega):
    along, across = scale * rate, scale * omega
    return along * d_re + across * d_im, along * d_im - across * d_re


def kernel(
    sizes,
    elev, equi, depth_in, mask_in, fric_in,
    out_e, out_f,
    E, Q, D, M, MI, F, AU, AV, V, S, FR, AX, PK, HT, PH,
    row_out, row_in, col_out, col_in,
    ring_out, ring_minus, ring_plus, ring_far,
    rs_minus, rs_plus, rs_far_a, rs_far_b,
    in_sem, halo_send, halo_recv, ring_send, ring_recv, red_send, red_recv,
):
    rows_dev, tiles, n_cons, n_ty, n_tx = sizes
    blocks = rows_dev // 8
    per_chunk = blocks // CHUNKS
    chunk_rows = 8 * per_chunk
    half = chunk_rows // 2
    last_row = PAD + rows_dev
    overlap = rows_dev - LANES

    c = lax.axis_index("cons")
    ty = lax.axis_index("ty")
    tx = lax.axis_index("tx")
    cp, cm, co = lax.rem(c + 1, n_cons), lax.rem(c + n_cons - 1, n_cons), lax.rem(c + 2, n_cons)
    north, south = lax.rem(ty + 1, n_ty), lax.rem(ty + n_ty - 1, n_ty)
    east, west = lax.rem(tx + 1, n_tx), lax.rem(tx + n_tx - 1, n_tx)

    loads = []
    for t in (0, tiles - 1) + tuple(range(1, tiles - 1)):
        lanes = pl.ds(LANES * t, LANES)
        inner = pl.ds(PAD, rows_dev)
        loads += [
            pltpu.make_async_copy(elev.at[:, :, :, lanes], E.at[:, :, t, inner, :], in_sem.at[5 * t]),
            pltpu.make_async_copy(equi.at[:, :, :, lanes], Q.at[:, :, t, inner, :], in_sem.at[5 * t + 1]),
            pltpu.make_async_copy(fric_in.at[:, lanes], F.at[t, inner, :], in_sem.at[5 * t + 2]),
            pltpu.make_async_copy(depth_in.at[:, lanes], D.at[t, inner, :], in_sem.at[5 * t + 3]),
            pltpu.make_async_copy(mask_in.at[:, lanes], MI.at[t], in_sem.at[5 * t + 4]),
        ]
    for load in loads:
        load.start()

    barrier = pltpu.get_barrier_semaphore()
    for there in ({"cons": cp}, {"cons": cm}, {"ty": north}, {"ty": south}, {"tx": east}, {"tx": west}):
        pl.semaphore_signal(barrier, inc=1, device_id=there, device_id_type=MESH)

    omegas = []
    for k in range(2):
        omega = jnp.float32(OMEGA_TABLE[k])
        for group in range(1, n_cons):
            omega = jnp.where(c == group, jnp.float32(OMEGA_TABLE[2 * group + k]), omega)
        omegas.append(omega)

    first_row = ty * rows_dev
    AX[...] = latitude_factor(
        first_row + lax.broadcasted_iota(jnp.int32, (rows_dev, LANES), 0), rows_dev * n_ty
    )
    ax_across = [
        latitude_factor(
            first_row + overlap * h + lax.broadcasted_iota(jnp.int32, (1, LANES), 1), rows_dev * n_ty
        )
        for h in range(2)
    ]

    lane = lax.broadcasted_iota(jnp.int32, (8, LANES), 1)
    lane_0, lane_last = lane == 0, lane == LANES - 1

    for load in loads:
        load.wait()

    @pl.loop(0, blocks)
    def _(b):
        for t in range(tiles):
            M[t, pl.ds(PAD + 8 * b, 8), :] = MI[t, pl.ds(8 * b, 8), :].astype(jnp.float32)

    def plane_of(p, t, rows, extras):
        if p < 4:
            return E[p // 2, p % 2, t, rows, :] - Q[p // 2, p % 2, t, rows, :]
        return extras[p - 4][t, rows, :]

    def pack_columns(extras):
        count = 4 + len(extras)

        @pl.loop(0, blocks)
        def _(b):
            rows = pl.ds(PAD + 8 * b, 8)
            packed = jnp.zeros((8, LANES), jnp.float32)
            for p in range(count):
                first = plane_of(p, 0, rows, extras)
                last = plane_of(p, tiles - 1, rows, extras)
                packed = jnp.where(lane == p, pltpu.roll(first, p, 1) if p else first, packed)
                packed = jnp.where(lane == 8 + p, pltpu.roll(last, 9 + p, 1), packed)
            PK[pl.ds(8 * b, 8), :] = packed

    def transpose_columns(which):
        for h in range(2):
            turned = PK[overlap * h : overlap * h + LANES, :].T
            col_out[which, 0, h] = turned[0:8]
            col_out[which, 1, h] = turned[8:16]

    def pack_rows(which, extras):
        for t in range(tiles):
            for p in range(4 + len(extras)):
                row_out[which, 0, t, p : p + 1, :] = plane_of(p, t, pl.ds(PAD, 1), extras)
                row_out[which, 1, t, p : p + 1, :] = plane_of(p, t, pl.ds(last_row - 1, 1), extras)

    def halo_copies(which):
        copies = []
        for side, (source, target, there) in enumerate(
            (
                (col_out.at[which, 0], col_in.at[which, 1], {"tx": west}),
                (col_out.at[which, 1], col_in.at[which, 0], {"tx": east}),
                (row_out.at[which, 0], row_in.at[which, 1], {"ty": south}),
                (row_out.at[which, 1], row_in.at[which, 0], {"ty": north}),
            )
        ):
            copies.append(
                pltpu.make_async_remote_copy(
                    source, target, halo_send.at[4 * which + side], halo_recv.at[4 * which + side],
                    device_id=there, device_id_type=MESH,
                )
            )
        return copies

    pack_columns((F, D, M))
    transpose_columns(0)
    pack_rows(0, (F, D, M))
    pl.semaphore_wait(barrier, 6)
    halo_one = halo_copies(0)
    for copy in halo_one:
        copy.start()
    for copy in halo_one:
        copy.wait_recv()

    inside_north = jnp.where(ty == n_ty - 1, jnp.float32(0), jnp.float32(1))
    inside_south = jnp.where(ty == 0, jnp.float32(0), jnp.float32(1))
    for t in range(tiles):
        for side, row, keep in ((0, PAD - 1, inside_south), (1, last_row, inside_north)):
            line = pl.ds(row, 1)
            for p in range(4):
                E[p // 2, p % 2, t, line, :] = row_in[0, side, t, p : p + 1, :]
                Q[p // 2, p % 2, t, line, :] = jnp.zeros((1, LANES), jnp.float32)
            F[t, line, :] = row_in[0, side, t, 4:5, :]
            D[t, line, :] = row_in[0, side, t, 5:6, :]
            M[t, line, :] = row_in[0, side, t, 6:7, :] * keep

    def western_flow(h, which, rate):
        own, other = col_out.at[which, 0, h], col_in.at[which, 0, h]
        here, there = col_out.at[0, 0, h], col_in.at[0, 0, h]
        mask = here[6:7, :] * there[6:7, :]
        deep = 0.5 * (here[5:6, :] + there[5:6, :])
        scale = -mask * deep * ax_across[h]
        for k in range(2):
            over = scale / (rate * rate + omegas[k] * omegas[k])
            d_re = own[2 * k : 2 * k + 1, :] - other[2 * k : 2 * k + 1, :]
            d_im = own[2 * k + 1 : 2 * k + 2, :] - other[2 * k + 1 : 2 * k + 2, :]
            u_re, u_im = face_flow(d_re, d_im, rate, over, omegas[k])
            HT[h, 2 * k : 2 * k + 1, :] = u_re
            HT[h, 2 * k + 1 : 2 * k + 2, :] = u_im

    def turn_back():
        PH[0:LANES, :] = HT[0].T
        PH[LANES:rows_dev, :] = HT[1].T[LANES - overlap :]

    for h in range(2):
        HT[h] = jnp.zeros((LANES, LANES), jnp.float32)
        HT[h, 8:16, :] = col_in[0, 1, h]
        western_flow(h, 0, 0.5 * (col_out[0, 0, h, 4:5, :] + col_in[0, 0, h, 4:5, :]))
    turn_back()

    def eastern_views(values, beyond):
        rolled = [pltpu.roll(v, LANES - 1, 1) for v in values] + [beyond]
        return [jnp.where(lane_last, rolled[t + 1], rolled[t]) for t in range(tiles)]

    def both_inverses(ru, rv, au, av, omega):
        square = omega * omega
        du, dv = ru * ru + square, rv * rv + square
        inverse = 1.0 / (du * dv)
        return au * (dv * inverse), av * (du * inverse)

    def southern_flow(R, fresh):
        rows, rows_n = pl.ds(0, 8), pl.ds(1, 8)
        for t in range(tiles):
            if fresh:
                av = -(M[t, rows, :] * M[t, rows_n, :]) * (0.5 * (D[t, rows, :] + D[t, rows_n, :])) * AY_SCALE
                AV[t, rows, :] = av
            else:
                av = AV[t, rows, :]
            rv = 0.5 * (R[t, rows, :] + R[t, rows_n, :])
            for k in range(2):
                over = av / (rv * rv + omegas[k] * omegas[k])
                d = [
                    (E[k, p, t, rows_n, :] - Q[k, p, t, rows_n, :]) - (E[k, p, t, rows, :] - Q[k, p, t, rows, :])
                    for p in range(2)
                ]
                v = face_flow(d[0], d[1], rv, over, omegas[k])
                for p in range(2):
                    V[k, p, t, rows, :] = v[p]

    def sweep_block(b, R, fresh):
        rows, rows_n, rows_s = pl.ds(PAD + 8 * b, 8), pl.ds(PAD + 8 * b + 1, 8), pl.ds(PAD + 8 * b - 1, 8)
        rim = PH[pl.ds(8 * b, 8), :]
        ax = AX[pl.ds(8 * b, 8), :]

        def beyond(p):
            return pltpu.roll(rim, (2 * LANES - 1 - (8 + p)) % LANES, 1)

        rate = [R[t, rows, :] for t in range(tiles)]
        rate_east = eastern_views(rate, beyond(4))
        if fresh:
            deep = [D[t, rows, :] for t in range(tiles)]
            deep_east = eastern_views(deep, beyond(5))
            mask = [M[t, rows, :] for t in range(tiles)]
            mask_east = eastern_views(mask, beyond(6))
        au, av, ru, rv = [], [], [], []
        for t in range(tiles):
            if fresh:
                au.append(-(mask[t] * mask_east[t]) * (0.5 * (deep[t] + deep_east[t])) * ax)
                av.append(-(mask[t] * M[t, rows_n, :]) * (0.5 * (deep[t] + D[t, rows_n, :])) * AY_SCALE)
                AU[t, rows, :] = au[t]
                AV[t, rows, :] = av[t]
            else:
                au.append(AU[t, rows, :])
                av.append(AV[t, rows, :])
            ru.append(0.5 * (rate[t] + rate_east[t]))
            rv.append(0.5 * (rate[t] + R[t, rows_n, :]))
        squares = [None] * tiles
        theta_ax = THETA * ax
        for k in range(2):
            omega = omegas[k]
            eta = [[E[k, p, t, rows, :] for t in range(tiles)] for p in range(2)]
            quil = [[Q[k, p, t, rows, :] for t in range(tiles)] for p in range(2)]
            zeta = [[eta[p][t] - quil[p][t] for t in range(tiles)] for p in range(2)]
            zeta_east = [eastern_views(zeta[p], beyond(2 * k + p)) for p in range(2)]
            flow_u = [[], []]
            flow_v = [[], []]
            for t in range(tiles):
                over_u, over_v = both_inverses(ru[t], rv[t], au[t], av[t], omega)
                u = face_flow(
                    zeta_east[0][t] - zeta[0][t], zeta_east[1][t] - zeta[1][t], ru[t], over_u, omega
                )
                north_z = [E[k, p, t, rows_n, :] - Q[k, p, t, rows_n, :] for p in range(2)]
                v = face_flow(north_z[0] - zeta[0][t], north_z[1] - zeta[1][t], rv[t], over_v, omega)
                for p in range(2):
                    flow_u[p].append(u[p])
                    flow_v[p].append(v[p])
                    V[k, p, t, rows, :] = v[p]
            west_u = []
            for p in range(2):
                q = 2 * k + p
                rolled = [pltpu.roll(rim, LANES - q, 1) if q else rim]
                rolled += [pltpu.roll(flow_u[p][t], 1, 1) for t in range(tiles)]
                west_u.append([jnp.where(lane_0, rolled[t], rolled[t + 1]) for t in range(tiles)])
            for t in range(tiles):
                south_v = [V[k, p, t, rows_s, :] for p in range(2)]
                for p in range(2):
                    turning = -omega * eta[1][t] if p == 0 else omega * eta[0][t]
                    change = (
                        THETA * turning
                        + theta_ax * (flow_u[p][t] - west_u[p][t])
                        + (THETA * AY_SCALE) * (flow_v[p][t] - south_v[p])
                    )
                    new = M[t, rows, :] * (eta[p][t] - change)
                    if fresh:
                        E[k, p, t, rows, :] = new
                        cu = flow_u[p][t] + west_u[p][t]
                        cv = flow_v[p][t] + south_v[p]
                        term = cu * cu + cv * cv
                        squares[t] = term if squares[t] is None else squares[t] + term
                    else:
                        out_e[k, p, pl.ds(8 * b, 8), LANES * t : LANES * (t + 1)] = new
        for t in range(tiles):
            if fresh:
                S[t, rows, :] = squares[t]
            else:
                out_f[pl.ds(8 * b, 8), LANES * t : LANES * (t + 1)] = rate[t]

    def span(j, part):
        start = PAD + chunk_rows * j
        if part == "a":
            return pl.ds(start, half)
        if part == "b":
            return pl.ds(start + half, half)
        return pl.ds(start, chunk_rows)

    def buffer_span(j):
        return pl.ds(half * j, half)

    def remote(source, target, slot, there):
        return pltpu.make_async_remote_copy(
            source, target, red_send.at[slot], red_recv.at[slot], device_id={"cons": there}, device_id_type=MESH
        )

    sent = []
    far, near, gather, relay = {}, {}, {}, {}

    def reduce_first(j):
        far[j] = (
            remote(S.at[co, span(j, "a"), :], rs_far_a.at[buffer_span(j), :], 10 * j, cp),
            remote(S.at[co, span(j, "b"), :], rs_far_b.at[buffer_span(j), :], 10 * j + 1, cm),
        )
        near[j] = (
            remote(S.at[cp, span(j, "b"), :], rs_minus.at[1, buffer_span(j), :], 10 * j + 2, cp),
            remote(S.at[cm, span(j, "a"), :], rs_plus.at[0, buffer_span(j), :], 10 * j + 3, cm),
        )
        for copy in far[j] + near[j]:
            copy.start()

    def reduce_second(j):
        far[j][0].wait_recv()
        rs_far_a[buffer_span(j), :] = S[cp, span(j, "a"), :] + rs_far_a[buffer_span(j), :]
        far[j][1].wait_recv()
        rs_far_b[buffer_span(j), :] = S[cm, span(j, "b"), :] + rs_far_b[buffer_span(j), :]
        near[j] += (
            remote(rs_far_a.at[buffer_span(j), :], rs_minus.at[0, buffer_span(j), :], 10 * j + 4, cp),
            remote(rs_far_b.at[buffer_span(j), :], rs_plus.at[1, buffer_span(j), :], 10 * j + 5, cm),
        )
        for copy in near[j][2:]:
            copy.start()

    def gather_first(j):
        for copy in near[j]:
            copy.wait_recv()
        for h, part in enumerate("ab"):
            rows = span(j, part)
            total = S[c, rows, :] + rs_minus[h, buffer_span(j), :] + rs_plus[h, buffer_span(j), :]
            FR[c, rows, :] = rate_of(total, D[c, rows, :])
        gather[j] = (
            remote(FR.at[c, span(j, ""), :], FR.at[c, span(j, ""), :], 10 * j + 6, cp),
            remote(FR.at[c, span(j, ""), :], FR.at[c, span(j, ""), :], 10 * j + 7, cm),
        )
        for copy in gather[j]:
            copy.start()

    def gather_second(j):
        for copy in gather[j]:
            copy.wait_recv()
        relay[j] = (
            remote(FR.at[cm, span(j, "a"), :], FR.at[cm, span(j, "a"), :], 10 * j + 8, cp),
            remote(FR.at[cp, span(j, "b"), :], FR.at[cp, span(j, "b"), :], 10 * j + 9, cm),
        )
        for copy in relay[j]:
            copy.start()

    def gathered(j):
        for copy in relay[j]:
            copy.wait_recv()

    southern_flow(F, True)
    for j in range(CHUNKS):

        @pl.loop(per_chunk * j, per_chunk * (j + 1))
        def _(b):
            sweep_block(b, F, True)

        reduce_first(j)
        if j >= 1:
            reduce_second(j - 1)
        if j >= 2:
            gather_first(j - 2)

    pack_columns((S,))
    transpose_columns(1)
    pack_rows(1, (S,))
    halo_two = halo_copies(1)
    for copy in halo_two:
        copy.start()

    reduce_second(CHUNKS - 1)
    gather_first(CHUNKS - 2)
    for copy in halo_two:
        copy.wait_recv()
    for t in range(tiles):
        ring_out[t : t + 1, :] = row_in[1, 0, t, 4:5, :]
        ring_out[tiles + t : tiles + t + 1, :] = row_in[1, 1, t, 4:5, :]
    for h in range(2):
        ring_out[8 + h : 9 + h, :] = col_in[1, 0, h, 4:5, :]
        ring_out[10 + h : 11 + h, :] = col_in[1, 1, h, 4:5, :]
        ring_out[12 + h : 13 + h, :] = col_out[1, 0, h, 4:5, :]
    ring_out[14:16, :] = jnp.zeros((2, LANES), jnp.float32)

    def ring_remote(source, target, slot, there):
        return pltpu.make_async_remote_copy(
            source, target, ring_send.at[slot], ring_recv.at[slot], device_id={"cons": there}, device_id_type=MESH
        )

    ring = [ring_remote(ring_out, ring_minus, 0, cp), ring_remote(ring_out, ring_plus, 1, cm)]
    for copy in ring:
        copy.start()
    gather_first(CHUNKS - 1)
    ring[0].wait_recv()
    ring.append(ring_remote(ring_minus, ring_far, 2, cp))
    ring[2].start()
    for j in range(CHUNKS):
        gather_second(j)
    ring[1].wait_recv()
    ring[2].wait_recv()

    def ring_rate(line, depth):
        rows = slice(line, line + 1)
        total = (ring_out[rows, :] + ring_minus[rows, :]) + (ring_plus[rows, :] + ring_far[rows, :])
        return rate_of(total, depth)

    for t in range(tiles):
        for side, row in ((0, PAD - 1), (1, last_row)):
            line = pl.ds(row, 1)
            for p in range(4):
                E[p // 2, p % 2, t, line, :] = row_in[1, side, t, p : p + 1, :]
            FR[t, line, :] = ring_rate(tiles * side + t, row_in[0, side, t, 5:6, :])
    for h in range(2):
        rate_west = ring_rate(8 + h, col_in[0, 0, h, 5:6, :])
        rate_east = ring_rate(10 + h, col_in[0, 1, h, 5:6, :])
        rate_own = ring_rate(12 + h, col_out[0, 0, h, 5:6, :])
        HT[h, 8:12, :] = col_in[1, 1, h, 0:4, :]
        HT[h, 12:13, :] = rate_east
        western_flow(h, 1, 0.5 * (rate_own + rate_west))
    turn_back()

    gathered(0)
    southern_flow(FR, False)
    for j in range(CHUNKS):
        if j + 1 < CHUNKS:
            gathered(j + 1)

        @pl.loop(per_chunk * j, per_chunk * (j + 1))
        def _(b):
            sweep_block(b, FR, False)

    for copy in halo_one + halo_two + ring:
        copy.wait_send()
    for j in range(CHUNKS):
        for copy in far[j] + near[j] + gather[j] + relay[j]:
            copy.wait_send()


def solution(mesh):
    n_cons, n_ty, n_tx = (mesh.shape[axis] for axis in ("cons", "ty", "tx"))

    def body(elevation, equilibrium, depth, land_mask, friction_prev):
        kdev, two, rows_dev, cols_dev = elevation.shape
        tiles = cols_dev // LANES
        tall = rows_dev + 2 * PAD
        f32 = jnp.float32
        field = pltpu.VMEM((tiles, tall, LANES), f32)
        fields = pltpu.VMEM((2, 2, tiles, tall, LANES), f32)
        half_rows = rows_dev // 2
        hbm = pl.BlockSpec(memory_space=pltpu.HBM)
        vmem = pl.BlockSpec(memory_space=pltpu.VMEM)
        return pl.pallas_call(
            functools.partial(kernel, (rows_dev, tiles, n_cons, n_ty, n_tx)),
            out_shape=(
                jax.ShapeDtypeStruct(elevation.shape, f32),
                jax.ShapeDtypeStruct(depth.shape, f32),
            ),
            in_specs=[hbm] * 5,
            out_specs=(vmem, vmem),
            scratch_shapes=[
                fields, fields, field, field,
                pltpu.VMEM((tiles, rows_dev, LANES), jnp.int32),
                field, field, field, fields, field, field,
                pltpu.VMEM((rows_dev, LANES), f32),
                pltpu.VMEM((rows_dev, LANES), f32),
                pltpu.VMEM((2, LANES, LANES), f32),
                pltpu.VMEM((rows_dev, LANES), f32),
                pltpu.VMEM((2, 2, tiles, 8, LANES), f32),
                pltpu.VMEM((2, 2, tiles, 8, LANES), f32),
                pltpu.VMEM((2, 2, 2, 8, LANES), f32),
                pltpu.VMEM((2, 2, 2, 8, LANES), f32),
                pltpu.VMEM((16, LANES), f32),
                pltpu.VMEM((16, LANES), f32),
                pltpu.VMEM((16, LANES), f32),
                pltpu.VMEM((16, LANES), f32),
                pltpu.VMEM((2, half_rows, LANES), f32),
                pltpu.VMEM((2, half_rows, LANES), f32),
                pltpu.VMEM((half_rows, LANES), f32),
                pltpu.VMEM((half_rows, LANES), f32),
                pltpu.SemaphoreType.DMA((5 * tiles,)),
                pltpu.SemaphoreType.DMA((8,)),
                pltpu.SemaphoreType.DMA((8,)),
                pltpu.SemaphoreType.DMA((3,)),
                pltpu.SemaphoreType.DMA((3,)),
                pltpu.SemaphoreType.DMA((10 * CHUNKS,)),
                pltpu.SemaphoreType.DMA((10 * CHUNKS,)),
            ],
            compiler_params=pltpu.CompilerParams(collective_id=0, has_side_effects=True),
        )(elevation, equilibrium, depth, land_mask, friction_prev)

    tiled = P("ty", "tx")
    planes = P("cons", None, "ty", "tx")
    return jax.shard_map(
        body,
        mesh=mesh,
        in_specs=(planes, planes, tiled, tiled, tiled),
        out_specs=(planes, tiled),
        check_vma=False,
    )
```

time: 137 us -> 48.2 us (0.35)
  the two profiles are of different devices: /device:TPU:1 before, /device:TPU:6 now
where the time goes in v1:
time: 48.2 us; the launch traced here: 47.5 us
  Pallas kernels  43.7 us (91%)
  local copies, waits for them, and re-layouts  3.13 us (6%)
  between operations  0.65 us (1%)
    pallas_call x1, Pallas kernels, body(): pl.pallas_call(functools.partial(kernel, (rows_dev, tiles, n_cons, n_ty,...  43.7 us
    unnamed x4, local copies, waits for them, and re-layouts  3.13 us

profile of v1, /device:TPU:6, one launch (start us, length us, event | category | flops | bytes accessed | tf_op | source)
XLA Modules:
  0.0 47.5 jit_solution(11330297887604519297)
XLA Ops:
  0.6 43.7 %shard_map.68 = (f32[2,2,144,512]{3,2,1,0:T(8,128)}, f32[144,512]{1,0:T(8,128)}) custom-call(f32[2,2,144,512]{3,2,1,0:T(8,128)} %elev.1, f32[2,2,144,512]{3,2,1,0:T(8,128)} %equi.1, f32[144,512]{1,0:T(8,128)} %depth_in.1, s32[144,512]{1,0:T(8,128)} %mask_in.1, f32[144,512]{1,0:T(8,128)} %fric_in.1), custom_call_target="tpu_custom_call" | custom-call | tf_op jit(solution)/shard_map/pallas_call | solution.py:483
  44.4 0.0 copy-start
  44.4 2.4 %copy.9 = f32[2,2,144,512]{3,2,1,0:T(8,128)} copy(f32[2,2,144,512]{3,2,1,0:T(8,128)} %get-tuple-element.4) | data formatting | bytes 2359296
  46.8 0.0 copy-done
  46.8 0.7 %copy.10 = f32[144,512]{1,0:T(8,128)} copy(f32[144,512]{1,0:T(8,128)S(1)} %copy-done) | data formatting | bytes 589824
Async XLA Ops:
  44.4 2.4 %copy-start = (f32[144,512]{1,0:T(8,128)S(1)}, f32[144,512]{1,0:T(8,128)}, u32[]{:S(2)}) copy-start(f32[144,512]{1,0:T(8,128)} %get-tuple-element.5) | copy-start | bytes 884740

commit v2 on v1

v2 whole, which is shorter than its diff:
```python
import functools
import math

import jax
import jax.numpy as jnp
from jax import lax
from jax.experimental import pallas as pl
from jax.experimental.pallas import tpu as pltpu
from jax.sharding import PartitionSpec as P

OMEGA_TABLE = (1.0, 1.0351, 0.9582, 1.0379, 0.5181, 0.4816, 0.5164, 0.4454)
AY_SCALE = 0.5
THETA = 0.05
DRAG = 0.5
BACKGROUND = 0.01

MESH = pl.DeviceIdType.MESH
LANES = 128
PAD = 8
FAR_FIRST = (2, 1, 3)
INNER = ((1, 9), (9, 17))
OUTER = ((0, 12), (12, 18))


def latitude_factor(rows, total):
    lat = (-60.0 + 120.0 * (rows.astype(jnp.float32) + 0.5) / total) * (math.pi / 180.0)
    return 0.5 / jnp.cos(lat)


def rate_of(total, depth):
    inverse = 1.0 / depth
    return DRAG * jnp.sqrt(0.125 * total * (inverse * inverse) + BACKGROUND) * inverse


def face_flow(d_re, d_im, rate, scale, omega):
    along, across = scale * rate, scale * omega
    return along * d_re + across * d_im, along * d_im - across * d_re


def kernel(
    sizes,
    elev, equi, depth_in, mask_in, fric_in,
    out_e, out_f,
    E, Q, E1, D, M, MI, F, AU, AV, U0, U2, V, S, FR, AX, PK, HT, PH,
    row_out, row_in, col_out, col_in, ring_out, ring_in, part_in,
    in_sem, halo_send, halo_recv, ring_send, ring_recv, part_send, part_recv, rate_send, rate_recv,
):
    rows_dev, tiles, n_cons, n_ty, n_tx = sizes
    blocks = rows_dev // 8
    last_row = PAD + rows_dev
    overlap = rows_dev - LANES
    inner_tiles, outer_tiles = tuple(range(1, tiles - 1)), (0, tiles - 1)

    c = lax.axis_index("cons")
    ty = lax.axis_index("ty")
    tx = lax.axis_index("tx")
    others = [lax.rem(c + d, n_cons) for d in range(1, n_cons)]
    owners = [lax.rem(c + n_cons - d, n_cons) for d in range(1, n_cons)]
    north, south = lax.rem(ty + 1, n_ty), lax.rem(ty + n_ty - 1, n_ty)
    east, west = lax.rem(tx + 1, n_tx), lax.rem(tx + n_tx - 1, n_tx)

    loads = []
    for t in outer_tiles + inner_tiles:
        lanes = pl.ds(LANES * t, LANES)
        within = pl.ds(PAD, rows_dev)
        loads += [
            pltpu.make_async_copy(elev.at[:, :, :, lanes], E.at[:, :, t, within, :], in_sem.at[5 * t]),
            pltpu.make_async_copy(equi.at[:, :, :, lanes], Q.at[:, :, t, within, :], in_sem.at[5 * t + 1]),
            pltpu.make_async_copy(fric_in.at[:, lanes], F.at[t, within, :], in_sem.at[5 * t + 2]),
            pltpu.make_async_copy(depth_in.at[:, lanes], D.at[t, within, :], in_sem.at[5 * t + 3]),
            pltpu.make_async_copy(mask_in.at[:, lanes], MI.at[t], in_sem.at[5 * t + 4]),
        ]
    for load in loads:
        load.start()

    barrier = pltpu.get_barrier_semaphore()
    met = [{"cons": other} for other in others]
    met += [{"ty": north}, {"ty": south}, {"tx": east}, {"tx": west}]
    for there in met:
        pl.semaphore_signal(barrier, inc=1, device_id=there, device_id_type=MESH)

    omegas = []
    for k in range(2):
        omega = jnp.float32(OMEGA_TABLE[k])
        for group in range(1, n_cons):
            omega = jnp.where(c == group, jnp.float32(OMEGA_TABLE[2 * group + k]), omega)
        omegas.append(omega)

    first_row = ty * rows_dev
    AX[...] = latitude_factor(
        first_row + lax.broadcasted_iota(jnp.int32, (rows_dev, LANES), 0), rows_dev * n_ty
    )
    ax_across = [
        latitude_factor(
            first_row + overlap * h + lax.broadcasted_iota(jnp.int32, (1, LANES), 1), rows_dev * n_ty
        )
        for h in range(2)
    ]

    lane = lax.broadcasted_iota(jnp.int32, (8, LANES), 1)
    lane_0, lane_last = lane == 0, lane == LANES - 1

    def arrive(tiles_now, copies):
        for load in copies:
            load.wait()

        @pl.loop(0, blocks, unroll=6)
        def _(b):
            for t in tiles_now:
                M[t, pl.ds(PAD + 8 * b, 8), :] = MI[t, pl.ds(8 * b, 8), :].astype(jnp.float32)

    arrive(outer_tiles, loads[:10])

    def plane_of(p, t, rows, eta, extras):
        if p < 4:
            return eta[p // 2, p % 2, t, rows, :] - Q[p // 2, p % 2, t, rows, :]
        return extras[p - 4][t, rows, :]

    def pack_columns(which, eta, extras):
        @pl.loop(0, blocks, unroll=6)
        def _(b):
            rows = pl.ds(PAD + 8 * b, 8)
            packed = jnp.zeros((8, LANES), jnp.float32)
            for p in range(4 + len(extras)):
                first = plane_of(p, 0, rows, eta, extras)
                last = plane_of(p, tiles - 1, rows, eta, extras)
                packed = jnp.where(lane == p, pltpu.roll(first, p, 1) if p else first, packed)
                packed = jnp.where(lane == 8 + p, pltpu.roll(last, 9 + p, 1), packed)
            PK[pl.ds(8 * b, 8), :] = packed

        for h in range(2):
            turned = PK[overlap * h : overlap * h + LANES, :].T
            col_out[which, 0, h] = turned[0:8]
            col_out[which, 1, h] = turned[8:16]

    def pack_rows(which, eta, extras):
        for t in range(tiles):
            for p in range(4 + len(extras)):
                row_out[which, 0, t, p : p + 1, :] = plane_of(p, t, pl.ds(PAD, 1), eta, extras)
                row_out[which, 1, t, p : p + 1, :] = plane_of(p, t, pl.ds(last_row - 1, 1), eta, extras)

    def halo_copies(which):
        copies = []
        for side, (source, target, there) in enumerate(
            (
                (col_out.at[which, 0], col_in.at[which, 1], {"tx": west}),
                (col_out.at[which, 1], col_in.at[which, 0], {"tx": east}),
                (row_out.at[which, 0], row_in.at[which, 1], {"ty": south}),
                (row_out.at[which, 1], row_in.at[which, 0], {"ty": north}),
            )
        ):
            copies.append(
                pltpu.make_async_remote_copy(
                    source, target, halo_send.at[4 * which + side], halo_recv.at[4 * which + side],
                    device_id=there, device_id_type=MESH,
                )
            )
        return copies

    groups = [(inner_tiles, a, (b - a) // 2, (b - a) // 2) for a, b in INNER] + [(inner_tiles, 0, 1, blocks - 1)]
    groups += [(outer_tiles, a, (b - a) // 2, (b - a) // 2) for a, b in OUTER]
    edges = len(INNER)

    def piece(g, owner):
        pair, first, count, step = groups[g]
        tile = pair[0] + (pair[1] - pair[0]) * (owner // 2)
        start = PAD + 8 * first + (8 * step) * lax.rem(owner, 2)
        return tile, pl.ds(pl.multiple_of(start, 8), 8 * count)

    def landing(g):
        start = 8 * sum(group[2] for group in groups[:g])
        return pl.ds(start, 8 * groups[g][2])

    def part_copy(g, d):
        tile, rows = piece(g, others[d - 1])
        return pltpu.make_async_remote_copy(
            S.at[tile, rows, :], part_in.at[d - 1, landing(g), :],
            part_send.at[g, d - 1], part_recv.at[g, d - 1],
            device_id={"cons": others[d - 1]}, device_id_type=MESH,
        )

    def rate_copy(g, d, source):
        tile, rows = piece(g, source)
        return pltpu.make_async_remote_copy(
            FR.at[tile, rows, :], FR.at[tile, rows, :],
            rate_send.at[g, d - 1], rate_recv.at[g, d - 1],
            device_id={"cons": others[d - 1]}, device_id_type=MESH,
        )

    def send_parts(g):
        for d in FAR_FIRST:
            part_copy(g, d).start()

    def settle(g):
        for d in FAR_FIRST:
            part_copy(g, d).wait_recv()
        tile, rows = piece(g, c)
        total = S[tile, rows, :]
        for d in FAR_FIRST:
            total = total + part_in[d - 1, landing(g), :]
        FR[tile, rows, :] = rate_of(total, D[tile, rows, :])
        for d in FAR_FIRST:
            rate_copy(g, d, c).start()

    def gathered(g):
        for d in FAR_FIRST:
            rate_copy(g, d, owners[d - 1]).wait_recv()

    def faces(mask, mask_next, deep, deep_next, scale):
        return -(mask * mask_next) * (0.5 * (deep + deep_next)) * scale

    def both_inverses(ru, rv, au, av, omega):
        square = omega * omega
        du, dv = ru * ru + square, rv * rv + square
        inverse = 1.0 / (du * dv)
        return au * (dv * inverse), av * (du * inverse)

    def northward(R, eta, fresh, start, which_tiles):
        rows, rows_n = pl.ds(start, 8), pl.ds(start + 1, 8)
        for t in which_tiles:
            if fresh:
                av = faces(M[t, rows, :], M[t, rows_n, :], D[t, rows, :], D[t, rows_n, :], AY_SCALE)
                AV[t, rows, :] = av
            else:
                av = AV[t, rows, :]
            rv = 0.5 * (R[t, rows, :] + R[t, rows_n, :])
            for k in range(2):
                over = av / (rv * rv + omegas[k] * omegas[k])
                d = [
                    (eta[k, p, t, rows_n, :] - Q[k, p, t, rows_n, :]) - (eta[k, p, t, rows, :] - Q[k, p, t, rows, :])
                    for p in range(2)
                ]
                v = face_flow(d[0], d[1], rv, over, omegas[k])
                for p in range(2):
                    V[k, p, t, rows, :] = v[p]

    def half_sweep(b, R, eta, fresh, inner):
        rows, rows_n, rows_s = pl.ds(PAD + 8 * b, 8), pl.ds(PAD + 8 * b + 1, 8), pl.ds(PAD + 8 * b - 1, 8)
        ax = AX[pl.ds(8 * b, 8), :]
        flowing = tuple(range(tiles - 1)) if inner else (tiles - 1,)
        closing = inner_tiles if inner else outer_tiles
        rim = None if inner else PH[pl.ds(8 * b, 8), :]

        def views(load, p):
            values = {t: load(t) for t in flowing}
            rolled = {t: pltpu.roll(values[t], LANES - 1, 1) for t in flowing}
            if inner:
                rolled[tiles - 1] = pltpu.roll(load(tiles - 1), LANES - 1, 1)
            else:
                rolled[tiles] = pltpu.roll(rim, (2 * LANES - 1 - (8 + p)) % LANES, 1)
            return values, {t: jnp.where(lane_last, rolled[t + 1], rolled[t]) for t in flowing}

        rate, rate_east = views(lambda t: R[t, rows, :], 4)
        if fresh:
            deep, deep_east = views(lambda t: D[t, rows, :], 5)
            mask, mask_east = views(lambda t: M[t, rows, :], 6)
        au, av, ru, rv = {}, {}, {}, {}
        for t in flowing:
            if fresh:
                au[t] = faces(mask[t], mask_east[t], deep[t], deep_east[t], ax)
                av[t] = faces(mask[t], M[t, rows_n, :], deep[t], D[t, rows_n, :], AY_SCALE)
                AU[t, rows, :] = au[t]
                AV[t, rows, :] = av[t]
            else:
                au[t] = AU[t, rows, :]
                av[t] = AV[t, rows, :]
            ru[t] = 0.5 * (rate[t] + rate_east[t])
            rv[t] = 0.5 * (rate[t] + R[t, rows_n, :])
        squares = {t: None for t in closing}
        theta_ax = THETA * ax
        for k in range(2):
            omega = omegas[k]
            theta_omega = THETA * omega
            zeta, zeta_east = [None, None], [None, None]
            for p in range(2):
                zeta[p], zeta_east[p] = views(lambda t: eta[k, p, t, rows, :] - Q[k, p, t, rows, :], 2 * k + p)
            flow_u, flow_v = [{}, {}], [{}, {}]
            for t in flowing:
                over_u, over_v = both_inverses(ru[t], rv[t], au[t], av[t], omega)
                u = face_flow(
                    zeta_east[0][t] - zeta[0][t], zeta_east[1][t] - zeta[1][t], ru[t], over_u, omega
                )
                north_z = [eta[k, p, t, rows_n, :] - Q[k, p, t, rows_n, :] for p in range(2)]
                v = face_flow(north_z[0] - zeta[0][t], north_z[1] - zeta[1][t], rv[t], over_v, omega)
                for p in range(2):
                    flow_u[p][t], flow_v[p][t] = u[p], v[p]
                    V[k, p, t, rows, :] = v[p]
            west_u = [{}, {}]
            for p in range(2):
                if inner:
                    rolled = {t: pltpu.roll(flow_u[p][t], 1, 1) for t in flowing}
                    U0[k, p, pl.ds(8 * b, 8), :] = flow_u[p][0]
                    U2[k, p, pl.ds(8 * b, 8), :] = rolled[tiles - 2]
                else:
                    q = 2 * k + p
                    flow_u[p][0] = U0[k, p, pl.ds(8 * b, 8), :]
                    flow_v[p][0] = V[k, p, 0, rows, :]
                    rolled = {t: pltpu.roll(flow_u[p][t], 1, 1) for t in closing}
                    rolled[-1] = pltpu.roll(rim, LANES - q, 1) if q else rim
                    rolled[tiles - 2] = U2[k, p, pl.ds(8 * b, 8), :]
                for t in closing:
                    west_u[p][t] = jnp.where(lane_0, rolled[t - 1], rolled[t])
            for t in closing:
                old = [eta[k, p, t, rows, :] for p in range(2)]
                wet = M[t, rows, :]
                for p in range(2):
                    south_v = V[k, p, t, rows_s, :]
                    turned = old[p] + theta_omega * old[1] if p == 0 else old[p] - theta_omega * old[0]
                    new = wet * (
                        turned
                        - theta_ax * (flow_u[p][t] - west_u[p][t])
                        - (THETA * AY_SCALE) * (flow_v[p][t] - south_v)
                    )
                    if fresh:
                        E1[k, p, t, rows, :] = new
                        cu = flow_u[p][t] + west_u[p][t]
                        cv = flow_v[p][t] + south_v
                        term = cu * cu + cv * cv
                        squares[t] = term if squares[t] is None else squares[t] + term
                    else:
                        out_e[k, p, pl.ds(8 * b, 8), LANES * t : LANES * (t + 1)] = new
        for t in closing:
            if fresh:
                S[t, rows, :] = squares[t]
            else:
                out_f[pl.ds(8 * b, 8), LANES * t : LANES * (t + 1)] = R[t, rows, :]

    def run(span, R, eta, fresh, inner):
        @pl.loop(span[0], span[1], unroll=next(u for u in (4, 3, 5, 2, 1) if (span[1] - span[0]) % u == 0))
        def _(b):
            half_sweep(b, R, eta, fresh, inner)

    pack_columns(0, E, (F, D, M))
    arrive(inner_tiles, loads[10:])
    pack_rows(0, E, (F, D, M))
    pl.semaphore_wait(barrier, len(met))
    halo_one = halo_copies(0)
    for copy in halo_one:
        copy.start()
    northward(F, E, True, PAD, inner_tiles)
    for g in (0, 1):
        run(INNER[g], F, E, True, True)
        send_parts(g)
    for copy in halo_one:
        copy.wait_recv()

    inside_north = jnp.where(ty == n_ty - 1, jnp.float32(0), jnp.float32(1))
    inside_south = jnp.where(ty == 0, jnp.float32(0), jnp.float32(1))
    for t in range(tiles):
        for side, row, keep in ((0, PAD - 1, inside_south), (1, last_row, inside_north)):
            line = pl.ds(row, 1)
            for p in range(4):
                E[p // 2, p % 2, t, line, :] = row_in[0, side, t, p : p + 1, :]
                Q[p // 2, p % 2, t, line, :] = jnp.zeros((1, LANES), jnp.float32)
            F[t, line, :] = row_in[0, side, t, 4:5, :]
            D[t, line, :] = row_in[0, side, t, 5:6, :]
            M[t, line, :] = row_in[0, side, t, 6:7, :] * keep

    def western_flow(h, which, rate):
        own, other = col_out.at[which, 0, h], col_in.at[which, 0, h]
        here, there = col_out.at[0, 0, h], col_in.at[0, 0, h]
        scale = faces(here[6:7, :], there[6:7, :], here[5:6, :], there[5:6, :], ax_across[h])
        for k in range(2):
            over = scale / (rate * rate + omegas[k] * omegas[k])
            d_re = own[2 * k : 2 * k + 1, :] - other[2 * k : 2 * k + 1, :]
            d_im = own[2 * k + 1 : 2 * k + 2, :] - other[2 * k + 1 : 2 * k + 2, :]
            u_re, u_im = face_flow(d_re, d_im, rate, over, omegas[k])
            HT[h, 2 * k : 2 * k + 1, :] = u_re
            HT[h, 2 * k + 1 : 2 * k + 2, :] = u_im

    def turn_back():
        PH[0:LANES, :] = HT[0].T
        PH[LANES:rows_dev, :] = HT[1].T[LANES - overlap :]

    for h in range(2):
        HT[h] = jnp.zeros((LANES, LANES), jnp.float32)
        HT[h, 8:16, :] = col_in[0, 1, h]
        western_flow(h, 0, 0.5 * (col_out[0, 0, h, 4:5, :] + col_in[0, 0, h, 4:5, :]))
    turn_back()
    northward(F, E, True, 0, range(tiles))
    for b in (0, blocks - 1):
        half_sweep(b, F, E, True, True)
    send_parts(edges)
    first_outer = edges + 1
    for i, span in enumerate(OUTER):
        run(span, F, E, True, False)
        send_parts(first_outer + i)

    pack_columns(1, E1, (S,))
    pack_rows(1, E1, (S,))
    halo_two = halo_copies(1)
    for copy in halo_two:
        copy.start()
    for g in range(first_outer):
        settle(g)
    settle(first_outer)
    for copy in halo_two:
        copy.wait_recv()
    for t in range(tiles):
        ring_out[t : t + 1, :] = row_in[1, 0, t, 4:5, :]
        ring_out[tiles + t : tiles + t + 1, :] = row_in[1, 1, t, 4:5, :]
    for h in range(2):
        ring_out[8 + h : 9 + h, :] = col_in[1, 0, h, 4:5, :]
        ring_out[10 + h : 11 + h, :] = col_in[1, 1, h, 4:5, :]
        ring_out[12 + h : 13 + h, :] = col_out[1, 0, h, 4:5, :]
    ring_out[14:16, :] = jnp.zeros((2, LANES), jnp.float32)
    ring = [
        pltpu.make_async_remote_copy(
            ring_out, ring_in.at[d - 1], ring_send.at[d - 1], ring_recv.at[d - 1],
            device_id={"cons": others[d - 1]}, device_id_type=MESH,
        )
        for d in range(1, n_cons)
    ]
    for copy in ring:
        copy.start()
    for g in range(first_outer + 1, len(groups)):
        settle(g)

    for g in (0, edges, first_outer):
        gathered(g)
    northward(FR, E1, False, PAD, inner_tiles)
    gathered(1)
    run((1, 11), FR, E1, False, True)
    gathered(first_outer + 1)
    run((11, 17), FR, E1, False, True)

    for copy in ring:
        copy.wait_recv()

    def ring_rate(line, depth):
        rows = slice(line, line + 1)
        total = (ring_out[rows, :] + ring_in[0, rows, :]) + (ring_in[1, rows, :] + ring_in[2, rows, :])
        return rate_of(total, depth)

    for t in range(tiles):
        for side, row in ((0, PAD - 1), (1, last_row)):
            line = pl.ds(row, 1)
            for p in range(4):
                E1[p // 2, p % 2, t, line, :] = row_in[1, side, t, p : p + 1, :]
            FR[t, line, :] = ring_rate(tiles * side + t, row_in[0, side, t, 5:6, :])
    for h in range(2):
        rate_west = ring_rate(8 + h, col_in[0, 0, h, 5:6, :])
        rate_east = ring_rate(10 + h, col_in[0, 1, h, 5:6, :])
        rate_own = ring_rate(12 + h, col_out[0, 0, h, 5:6, :])
        HT[h, 8:12, :] = col_in[1, 1, h, 0:4, :]
        HT[h, 12:13, :] = rate_east
        western_flow(h, 1, 0.5 * (rate_own + rate_west))
    turn_back()
    northward(FR, E1, False, 0, range(tiles))
    for b in (0, blocks - 1):
        half_sweep(b, FR, E1, False, True)
    run((0, blocks), FR, E1, False, False)

    for copy in halo_one + halo_two + ring:
        copy.wait_send()
    for g in range(len(groups)):
        for d in FAR_FIRST:
            part_copy(g, d).wait_send()
            rate_copy(g, d, c).wait_send()


def solution(mesh):
    n_cons, n_ty, n_tx = (mesh.shape[axis] for axis in ("cons", "ty", "tx"))

    def body(elevation, equilibrium, depth, land_mask, friction_prev):
        kdev, two, rows_dev, cols_dev = elevation.shape
        tiles = cols_dev // LANES
        tall = rows_dev + 2 * PAD
        f32 = jnp.float32
        field = pltpu.VMEM((tiles, tall, LANES), f32)
        fields = pltpu.VMEM((2, 2, tiles, tall, LANES), f32)
        n_groups = len(INNER) + len(OUTER) + 1
        hbm = pl.BlockSpec(memory_space=pltpu.HBM)
        vmem = pl.BlockSpec(memory_space=pltpu.VMEM)
        return pl.pallas_call(
            functools.partial(kernel, (rows_dev, tiles, n_cons, n_ty, n_tx)),
            out_shape=(
                pltpu.VMEM(elevation.shape, f32),
                pltpu.VMEM(depth.shape, f32),
            ),
            in_specs=[hbm] * 5,
            out_specs=(vmem, vmem),
            scratch_shapes=[
                fields, fields, fields, field, field,
                pltpu.VMEM((tiles, rows_dev, LANES), jnp.int32),
                field, field, field,
                pltpu.VMEM((2, 2, rows_dev, LANES), f32),
                pltpu.VMEM((2, 2, rows_dev, LANES), f32),
                fields, field, field,
                pltpu.VMEM((rows_dev, LANES), f32),
                pltpu.VMEM((rows_dev, LANES), f32),
                pltpu.VMEM((2, LANES, LANES), f32),
                pltpu.VMEM((rows_dev, LANES), f32),
                pltpu.VMEM((2, 2, tiles, 8, LANES), f32),
                pltpu.VMEM((2, 2, tiles, 8, LANES), f32),
                pltpu.VMEM((2, 2, 2, 8, LANES), f32),
                pltpu.VMEM((2, 2, 2, 8, LANES), f32),
                pltpu.VMEM((16, LANES), f32),
                pltpu.VMEM((n_cons - 1, 16, LANES), f32),
                pltpu.VMEM((n_cons - 1, rows_dev, LANES), f32),
                pltpu.SemaphoreType.DMA((5 * tiles,)),
                pltpu.SemaphoreType.DMA((8,)),
                pltpu.SemaphoreType.DMA((8,)),
                pltpu.SemaphoreType.DMA((n_cons - 1,)),
                pltpu.SemaphoreType.DMA((n_cons - 1,)),
                pltpu.SemaphoreType.DMA((n_groups, n_cons - 1)),
                pltpu.SemaphoreType.DMA((n_groups, n_cons - 1)),
                pltpu.SemaphoreType.DMA((n_groups, n_cons - 1)),
                pltpu.SemaphoreType.DMA((n_groups, n_cons - 1)),
            ],
            compiler_params=pltpu.CompilerParams(collective_id=0, has_side_effects=True, vmem_limit_bytes=56 * 2**20),
        )(elevation, equilibrium, depth, land_mask, friction_prev)

    tiled = P("ty", "tx")
    planes = P("cons", None, "ty", "tx")
    return jax.shard_map(
        body,
        mesh=mesh,
        in_specs=(planes, planes, tiled, tiled, tiled),
        out_specs=(planes, tiled),
        check_vma=False,
    )
```

time: 48.2 us -> 34.9 us (0.72); the launches traced: 47.5 us -> 34.8 us
  Pallas kernels: 43.7 us -> 32.4 us
  local copies, waits for them, and re-layouts: 3.13 us -> 1.73 us
    pallas_call x1, Pallas kernels: 43.7 us -> 32.4 us  [body(): pl.pallas_call(functools.partial(kernel, (rows_dev, tiles, n_cons, n_ty,...]
    unnamed x4 -> x2, local copies, waits for them, and re-layouts: 3.13 us -> 1.73 us
where the time goes in v2:
time: 34.9 us; the launch traced here: 34.8 us
  Pallas kernels  32.4 us (93%)
  local copies, waits for them, and re-layouts  1.73 us (5%)
  between operations  0.64 us (2%)
    pallas_call x1, Pallas kernels, body(): pl.pallas_call(functools.partial(kernel, (rows_dev, tiles, n_cons, n_ty,...  32.4 us
    unnamed x2, local copies, waits for them, and re-layouts  1.73 us

profile of v2, /device:TPU:6, one launch (start us, length us, event | category | flops | bytes accessed | tf_op | source)
XLA Modules:
  0.0 34.8 jit_solution(11463861824344306487)
XLA Ops:
  0.6 32.4 %shard_map.68 = (f32[2,2,144,512]{3,2,1,0:T(8,128)S(1)}, f32[144,512]{1,0:T(8,128)S(1)}) custom-call(f32[2,2,144,512]{3,2,1,0:T(8,128)} %elev.1, f32[2,2,144,512]{3,2,1,0:T(8,128)} %equi.1, f32[144,512]{1,0:T(8,128)} %depth_in.1, s32[144,512]{1,0:T(8,128)} %mask_in.1, f32[144,512]{1,0:T(8,128)} %fric_in.1), custom_call_target="tpu_custom_call" | custom-call | tf_op jit(solution)/shard_map/pallas_call | solution.py:475
  33.1 1.0 %copy.9 = f32[2,2,144,512]{3,2,1,0:T(8,128)} copy(f32[2,2,144,512]{3,2,1,0:T(8,128)S(1)} %get-tuple-element.2) | data formatting | bytes 2359296
  34.1 0.7 %copy.10 = f32[144,512]{1,0:T(8,128)} copy(f32[144,512]{1,0:T(8,128)S(1)} %get-tuple-element.3) | data formatting | bytes 589824

commit v3 on v2

--- a/solution.py
+++ b/solution.py
@@ -35,6 +35,10 @@
 def face_flow(d_re, d_im, rate, scale, omega):
     along, across = scale * rate, scale * omega
     return along * d_re + across * d_im, along * d_im - across * d_re
+
+
+def unroll_of(count):
+    return next((u for u in (4, 3, 5, 2) if count % u == 0), 1)
 
 
 def kernel(
@@ -59,6 +63,12 @@
     north, south = lax.rem(ty + 1, n_ty), lax.rem(ty + n_ty - 1, n_ty)
     east, west = lax.rem(tx + 1, n_tx), lax.rem(tx + n_tx - 1, n_tx)
 
+    barrier = pltpu.get_barrier_semaphore()
+    met = [{"cons": other} for other in others]
+    met += [{"ty": north}, {"ty": south}, {"tx": east}, {"tx": west}]
+    for there in met:
+        pl.semaphore_signal(barrier, inc=1, device_id=there, device_id_type=MESH)
+
     loads = []
     for t in outer_tiles + inner_tiles:
         lanes = pl.ds(LANES * t, LANES)
@@ -72,12 +82,6 @@
         ]
     for load in loads:
         load.start()
-
-    barrier = pltpu.get_barrier_semaphore()
-    met = [{"cons": other} for other in others]
-    met += [{"ty": north}, {"ty": south}, {"tx": east}, {"tx": west}]
-    for there in met:
-        pl.semaphore_signal(barrier, inc=1, device_id=there, device_id_type=MESH)
 
     omegas = []
     for k in range(2):
@@ -326,7 +330,7 @@
                 out_f[pl.ds(8 * b, 8), LANES * t : LANES * (t + 1)] = R[t, rows, :]
 
     def run(span, R, eta, fresh, inner):
-        @pl.loop(span[0], span[1], unroll=next(u for u in (4, 3, 5, 2, 1) if (span[1] - span[0]) % u == 0))
+        @pl.loop(span[0], span[1], unroll=unroll_of(span[1] - span[0]))
         def _(b):
             half_sweep(b, R, eta, fresh, inner)
 
@@ -421,8 +425,6 @@
     northward(FR, E1, False, PAD, inner_tiles)
     gathered(1)
     run((1, 11), FR, E1, False, True)
-    gathered(first_outer + 1)
-    run((11, 17), FR, E1, False, True)
 
     for copy in ring:
         copy.wait_recv()
@@ -447,9 +449,14 @@
         western_flow(h, 1, 0.5 * (rate_own + rate_west))
     turn_back()
     northward(FR, E1, False, 0, range(tiles))
-    for b in (0, blocks - 1):
-        half_sweep(b, FR, E1, False, True)
-    run((0, blocks), FR, E1, False, False)
+    half_sweep(0, FR, E1, False, True)
+    run((0, 3), FR, E1, False, False)
+    run((3, 11), FR, E1, False, False)
+    gathered(first_outer + 1)
+    run((11, 17), FR, E1, False, True)
+    half_sweep(blocks - 1, FR, E1, False, True)
+    run((11, 15), FR, E1, False, False)
+    run((15, blocks), FR, E1, False, False)
 
     for copy in halo_one + halo_two + ring:
         copy.wait_send()

time: 34.9 us -> 34.3 us (0.983)
  Pallas kernels: 32.4 us -> 31.8 us
    pallas_call x1, Pallas kernels: 32.4 us -> 31.8 us  [body(): pl.pallas_call(functools.partial(kernel, (rows_dev, tiles, n_cons, n_ty,...]
where the time goes in v3:
time: 34.3 us; the launch traced here: 34.1 us
  Pallas kernels  31.8 us (93%)
  local copies, waits for them, and re-layouts  1.73 us (5%)
  between operations  0.64 us (2%)
    pallas_call x1, Pallas kernels, body(): pl.pallas_call(functools.partial(kernel, (rows_dev, tiles, n_cons, n_ty,...  31.8 us
    unnamed x2, local copies, waits for them, and re-layouts  1.73 us

profile of v3, /device:TPU:6, one launch (start us, length us, event | category | flops | bytes accessed | tf_op | source)
XLA Modules:
  0.0 34.1 jit_solution(13736696380604590395)
XLA Ops:
  0.6 31.8 %shard_map.68 = (f32[2,2,144,512]{3,2,1,0:T(8,128)S(1)}, f32[144,512]{1,0:T(8,128)S(1)}) custom-call(f32[2,2,144,512]{3,2,1,0:T(8,128)} %elev.1, f32[2,2,144,512]{3,2,1,0:T(8,128)} %equi.1, f32[144,512]{1,0:T(8,128)} %depth_in.1, s32[144,512]{1,0:T(8,128)} %mask_in.1, f32[144,512]{1,0:T(8,128)} %fric_in.1), custom_call_target="tpu_custom_call" | custom-call | tf_op jit(solution)/shard_map/pallas_call | solution.py:482
  32.4 1.0 %copy.9 = f32[2,2,144,512]{3,2,1,0:T(8,128)} copy(f32[2,2,144,512]{3,2,1,0:T(8,128)S(1)} %get-tuple-element.2) | data formatting | bytes 2359296
  33.4 0.7 %copy.10 = f32[144,512]{1,0:T(8,128)} copy(f32[144,512]{1,0:T(8,128)S(1)} %get-tuple-element.3) | data formatting | bytes 589824

commit v4 on v3

--- a/solution.py
+++ b/solution.py
@@ -345,7 +345,31 @@
     for g in (0, 1):
         run(INNER[g], F, E, True, True)
         send_parts(g)
-    for copy in halo_one:
+    for copy in halo_one[:2]:
+        copy.wait_recv()
+
+    def western_flow(h, which, rate):
+        own, other = col_out.at[which, 0, h], col_in.at[which, 0, h]
+        here, there = col_out.at[0, 0, h], col_in.at[0, 0, h]
+        scale = faces(here[6:7, :], there[6:7, :], here[5:6, :], there[5:6, :], ax_across[h])
+        for k in range(2):
+            over = scale / (rate * rate + omegas[k] * omegas[k])
+            d_re = own[2 * k : 2 * k + 1, :] - other[2 * k : 2 * k + 1, :]
+            d_im = own[2 * k + 1 : 2 * k + 2, :] - other[2 * k + 1 : 2 * k + 2, :]
+            u_re, u_im = face_flow(d_re, d_im, rate, over, omegas[k])
+            HT[h, 2 * k : 2 * k + 1, :] = u_re
+            HT[h, 2 * k + 1 : 2 * k + 2, :] = u_im
+
+    def turn_back():
+        PH[0:LANES, :] = HT[0].T
+        PH[LANES:rows_dev, :] = HT[1].T[LANES - overlap :]
+
+    for h in range(2):
+        HT[h] = jnp.zeros((LANES, LANES), jnp.float32)
+        HT[h, 8:16, :] = col_in[0, 1, h]
+        western_flow(h, 0, 0.5 * (col_out[0, 0, h, 4:5, :] + col_in[0, 0, h, 4:5, :]))
+    turn_back()
+    for copy in halo_one[2:]:
         copy.wait_recv()
 
     inside_north = jnp.where(ty == n_ty - 1, jnp.float32(0), jnp.float32(1))
@@ -359,28 +383,6 @@
             F[t, line, :] = row_in[0, side, t, 4:5, :]
             D[t, line, :] = row_in[0, side, t, 5:6, :]
             M[t, line, :] = row_in[0, side, t, 6:7, :] * keep
-
-    def western_flow(h, which, rate):
-        own, other = col_out.at[which, 0, h], col_in.at[which, 0, h]
-        here, there = col_out.at[0, 0, h], col_in.at[0, 0, h]
-        scale = faces(here[6:7, :], there[6:7, :], here[5:6, :], there[5:6, :], ax_across[h])
-        for k in range(2):
-            over = scale / (rate * rate + omegas[k] * omegas[k])
-            d_re = own[2 * k : 2 * k + 1, :] - other[2 * k : 2 * k + 1, :]
-            d_im = own[2 * k + 1 : 2 * k + 2, :] - other[2 * k + 1 : 2 * k + 2, :]
-            u_re, u_im = face_flow(d_re, d_im, rate, over, omegas[k])
-            HT[h, 2 * k : 2 * k + 1, :] = u_re
-            HT[h, 2 * k + 1 : 2 * k + 2, :] = u_im
-
-    def turn_back():
-        PH[0:LANES, :] = HT[0].T
-        PH[LANES:rows_dev, :] = HT[1].T[LANES - overlap :]
-
-    for h in range(2):
-        HT[h] = jnp.zeros((LANES, LANES), jnp.float32)
-        HT[h, 8:16, :] = col_in[0, 1, h]
-        western_flow(h, 0, 0.5 * (col_out[0, 0, h, 4:5, :] + col_in[0, 0, h, 4:5, :]))
-    turn_back()
     northward(F, E, True, 0, range(tiles))
     for b in (0, blocks - 1):
         half_sweep(b, F, E, True, True)
@@ -390,10 +392,12 @@
         run(span, F, E, True, False)
         send_parts(first_outer + i)
 
+    halo_two = halo_copies(1)
+    pack_rows(1, E1, (S,))
+    for copy in halo_two[2:]:
+        copy.start()
     pack_columns(1, E1, (S,))
-    pack_rows(1, E1, (S,))
-    halo_two = halo_copies(1)
-    for copy in halo_two:
+    for copy in halo_two[:2]:
         copy.start()
     for g in range(first_outer):
         settle(g)

time: 34.3 us -> 34.3 us (level)
  no operation moved by 1% of the time
where the time goes in v4:
time: 34.3 us; the launch traced here: 34.2 us
  Pallas kernels  31.8 us (93%)
  local copies, waits for them, and re-layouts  1.73 us (5%)
  between operations  0.64 us (2%)
    pallas_call x1, Pallas kernels, body(): pl.pallas_call(functools.partial(kernel, (rows_dev, tiles, n_cons, n_ty,...  31.8 us
    unnamed x2, local copies, waits for them, and re-layouts  1.73 us

profile of v4, /device:TPU:6, one launch (start us, length us, event | category | flops | bytes accessed | tf_op | source)
XLA Modules:
  0.0 34.2 jit_solution(16473524301806331038)
XLA Ops:
  0.6 31.8 %shard_map.68 = (f32[2,2,144,512]{3,2,1,0:T(8,128)S(1)}, f32[144,512]{1,0:T(8,128)S(1)}) custom-call(f32[2,2,144,512]{3,2,1,0:T(8,128)} %elev.1, f32[2,2,144,512]{3,2,1,0:T(8,128)} %equi.1, f32[144,512]{1,0:T(8,128)} %depth_in.1, s32[144,512]{1,0:T(8,128)} %mask_in.1, f32[144,512]{1,0:T(8,128)} %fric_in.1), custom_call_target="tpu_custom_call" | custom-call | tf_op jit(solution)/shard_map/pallas_call | solution.py:486
  32.5 1.0 %copy.9 = f32[2,2,144,512]{3,2,1,0:T(8,128)} copy(f32[2,2,144,512]{3,2,1,0:T(8,128)S(1)} %get-tuple-element.2) | data formatting | bytes 2359296
  33.5 0.7 %copy.10 = f32[144,512]{1,0:T(8,128)} copy(f32[144,512]{1,0:T(8,128)S(1)} %get-tuple-element.3) | data formatting | bytes 589824

commit v5 on v4

--- a/solution.py
+++ b/solution.py
@@ -470,6 +470,17 @@
             rate_copy(g, d, c).wait_send()
 
 
+def put_out(e_ref, f_ref, e_out, f_out, sem):
+    copies = [
+        pltpu.make_async_copy(e_ref.at[k, p], e_out.at[k, p], sem.at[2 * k + p]) for k in range(2) for p in range(2)
+    ]
+    copies.append(pltpu.make_async_copy(f_ref, f_out, sem.at[4]))
+    for copy in copies:
+        copy.start()
+    for copy in copies:
+        copy.wait()
+
+
 def solution(mesh):
     n_cons, n_ty, n_tx = (mesh.shape[axis] for axis in ("cons", "ty", "tx"))
 
@@ -483,7 +494,7 @@
         n_groups = len(INNER) + len(OUTER) + 1
         hbm = pl.BlockSpec(memory_space=pltpu.HBM)
         vmem = pl.BlockSpec(memory_space=pltpu.VMEM)
-        return pl.pallas_call(
+        moved = pl.pallas_call(
             functools.partial(kernel, (rows_dev, tiles, n_cons, n_ty, n_tx)),
             out_shape=(
                 pltpu.VMEM(elevation.shape, f32),
@@ -521,6 +532,17 @@
             ],
             compiler_params=pltpu.CompilerParams(collective_id=0, has_side_effects=True, vmem_limit_bytes=56 * 2**20),
         )(elevation, equilibrium, depth, land_mask, friction_prev)
+        return pl.pallas_call(
+            put_out,
+            out_shape=(
+                jax.ShapeDtypeStruct(elevation.shape, f32),
+                jax.ShapeDtypeStruct(depth.shape, f32),
+            ),
+            in_specs=[pl.BlockSpec(memory_space=pl.ANY)] * 2,
+            out_specs=(hbm, hbm),
+            scratch_shapes=[pltpu.SemaphoreType.DMA((5,))],
+            compiler_params=pltpu.CompilerParams(vmem_limit_bytes=8 * 2**20),
+        )(*moved)
 
     tiled = P("ty", "tx")
     planes = P("cons", None, "ty", "tx")

time: 34.3 us -> 33.8 us (0.985)
  local copies, waits for them, and re-layouts: 1.73 us -> 0 us
  Pallas kernels: 31.8 us -> 33 us
    unnamed x2 -> x0, local copies, waits for them, and re-layouts: 1.73 us -> none
    pallas_call x0 -> x1, Pallas kernels: none -> 1.15 us  [body(): pl.pallas_call(put_out, out_shape=(jax.ShapeDtypeStruct(elevation.shape,...]
where the time goes in v5:
time: 33.8 us; the launch traced here: 33.6 us
  Pallas kernels  33 us (98%)
  between operations  0.64 us (2%)
    pallas_call x1, Pallas kernels, body(): pl.pallas_call(functools.partial(kernel, (rows_dev, tiles, n_cons, n_ty,...  31.8 us
    pallas_call x1, Pallas kernels, body(): pl.pallas_call(put_out, out_shape=(jax.ShapeDtypeStruct(elevation.shape,...  1.15 us

profile of v5, /device:TPU:6, one launch (start us, length us, event | category | flops | bytes accessed | tf_op | source)
XLA Modules:
  0.0 33.6 jit_solution(4347591329596291285)
XLA Ops:
  0.6 31.8 %shard_map.68 = (f32[2,2,144,512]{3,2,1,0:T(8,128)S(1)}, f32[144,512]{1,0:T(8,128)S(1)}) custom-call(f32[2,2,144,512]{3,2,1,0:T(8,128)} %elev.1, f32[2,2,144,512]{3,2,1,0:T(8,128)} %equi.1, f32[144,512]{1,0:T(8,128)} %depth_in.1, s32[144,512]{1,0:T(8,128)} %mask_in.1, f32[144,512]{1,0:T(8,128)} %fric_in.1), custom_call_target="tpu_custom_call" | custom-call | tf_op jit(solution)/shard_map/pallas_call | solution.py:497
  32.5 1.1 %shard_map.69 = (f32[2,2,144,512]{3,2,1,0:T(8,128)}, f32[144,512]{1,0:T(8,128)}) custom-call(f32[2,2,144,512]{3,2,1,0:T(8,128)S(1)} %get-tuple-element.4.e_ref, f32[144,512]{1,0:T(8,128)S(1)} %get-tuple-element.5.f_ref), custom_call_target="tpu_custom_call" | custom-call | tf_op jit(solution)/shard_map/pallas_call | solution.py:535
